TPU v7x, 32 devices: a whole 2x2x4 slice. The times are simulated.
32 devices in a mesh: wave: 8 (over z, y), lev: 4 (over x, core).
Axes of the slice: x: 2, y: 2, z: 4, core: 2. Of those that a mesh axis runs over, the one named last changes fastest.
Arguments:
- spectral: float32 [8, 136, 2, 1280], P('wave', 'lev'), may hold values from -6 to 6
- to_modes: float32 [136, 136], replicated
- from_modes: float32 [136, 136], replicated
- mode_depths: float32 [136], replicated, may hold values from 0.05 to 5
- legendre: float32 [8, 16, 1280], P('wave'), may hold values from -0.03125 to 0.03125
- wave_ids: int32 [8], replicated, may hold values from 0 to 1279, as said below
- lat_points: int32 [16], P('wave'), may hold values from 20 to 5136, as said below
Outputs:
- grid: float32 [136, 16, 5136], P('lev', 'wave')
Inputs may be any that keep to these rules, and one draw needn't show every extreme that they name: `wave_ids`: distinct and ascending; 0 and 1279 are always among them. `lat_points`: each is 20 + 4 k for a whole k; not falling along the latitudes; the last is always 5136.
All inputs are finite; a program needn't handle non-finite values.
Results may differ from a plain program's by a relative error of at most 0.0003.
Values sent between devices are 32-bit elements; how exact they have to be, the bound alone decides.
No kernel may reach another device: no remote copies, remote signals or barrier semaphores. Data moves between devices by JAX's collectives and lax.ppermute only.
A program may use at most 64 MiB of HBM per device.

v0:
```python
import math
import jax
import jax.numpy as jnp
from jax import lax
from jax.sharding import PartitionSpec as P

LONS = 5136
two_pi = 2.0 * math.pi


def on_device(spectral, to_modes, from_modes, mode_depths, legendre, wave_ids, lat_points):
    highest = lax.Precision.HIGHEST
    waves_here = spectral.shape[0]
    total_orders = spectral.shape[3]
    block_len = total_orders // lax.axis_size("lev")
    columns = lax.all_to_all(spectral, "lev", split_axis=3, concat_axis=1, tiled=True)
    mode_coeffs = jnp.einsum("kl,wlcn->wkcn", to_modes, columns, precision=highest)
    first_order = lax.axis_index("lev") * block_len
    order_ids = first_order + jnp.arange(block_len)
    orders = order_ids.astype(jnp.float32)
    damping = 1.0 + mode_depths[:, None] * (orders * (orders + 1.0))[None, :] / float(
        total_orders * total_orders
    )
    divergence = jnp.einsum(
        "lk,wkcn->wlcn", from_modes, mode_coeffs / damping[None, :, None, :], precision=highest
    )
    own_ids = lax.dynamic_slice_in_dim(wave_ids, lax.axis_index("wave") * waves_here, waves_here)
    level_major = lax.all_to_all(divergence, "lev", split_axis=1, concat_axis=3, tiled=True)
    keep_mask = (jnp.arange(total_orders)[None, :] >= own_ids[:, None]).astype(jnp.float32)
    fourier = jnp.einsum(
        "wjn,wlcn->lwcj", legendre * keep_mask[:, None, :], level_major, precision=highest
    )
    band_data = lax.all_to_all(fourier, "wave", split_axis=3, concat_axis=1, tiled=True)
    positions = jnp.arange(LONS)

    def one_row(inputs):
        coeffs, points = inputs
        residue = wave_ids[:, None] * positions[None, :] % points
        phases = jnp.float32(two_pi) * residue.astype(jnp.float32) / points.astype(jnp.float32)
        weight = jnp.where(2 * wave_ids < points, jnp.where(wave_ids == 0, 1.0, 2.0), 0.0).astype(
            jnp.float32
        )
        basis_table = jnp.concatenate(
            [jnp.cos(phases) * weight[:, None], jnp.sin(phases) * weight[:, None]], 0
        )
        coefficient = jnp.concatenate([coeffs[:, :, 0], -coeffs[:, :, 1]], 1)
        lat_row = jnp.dot(coefficient, basis_table, precision=highest)
        return lat_row * (positions < points).astype(jnp.float32)[None, :]

    lat_rows = lax.map(one_row, (jnp.moveaxis(band_data, 3, 0), lat_points))
    return jnp.transpose(lat_rows, (1, 0, 2))


def solution(mesh):
    return jax.shard_map(
        on_device,
        mesh=mesh,
        in_specs=(
            P("wave", "lev", None, None),
            P(),
            P(),
            P(),
            P("wave", None, None),
            P(),
            P("wave"),
        ),
        out_specs=P("lev", "wave", None),
        check_vma=False,
    )
```

profile of v0, /device:TPU:0, one launch (start us, length us, event | category | flops | bytes accessed | tf_op | source)
XLA Modules:
  0.0 79.2 jit_solution(634367973494513038)
XLA Ops:
  0.0 2.6 %copy.29 = f32[1,34,2,1280]{1,2,0,3:T(2,128)S(1)} copy(f32[1,34,2,1280]{3,2,1,0:T(2,128)} %param.9) | data formatting | bytes 696320 | tf_op args[0]
  2.7 3.0 %reshape.90 = f32[4,1,21760]{2,1,0:T(1,128)} reshape(f32[1280,1,2,34]{3,2,1,0:T(2,128)S(1)} %bitcast.71) | data formatting | bytes 696320
  5.7 4.2 %all-to-all-start = ((f32[4,1,21760]{2,1,0:T(1,128)}), f32[4,1,21760]{2,1,0:T(1,128)S(1)}, u32[]{:S(2)}, u32[]{:S(2)}) async-start(f32[4,1,21760]{2,1,0:T(1,128)} %reshape.90), calls=%async_computation | async-start | bytes 696320 | tf_op jit(solution)/shard_map/all_to_all | solution.py:16
  10.0 6.9 %all-to-all-done = f32[4,1,21760]{2,1,0:T(1,128)S(1)} async-done(((f32[4,1,21760]{2,1,0:T(1,128)}), f32[4,1,21760]{2,1,0:T(1,128)S(1)}, u32[]{:S(2)}, u32[]{:S(2)}) %all-to-all-start) | async-done | bytes 348192 | tf_op jit(solution)/shard_map/all_to_all | solution.py:16
  17.4 1.6 %reduce = f32[4,21760]{1,0:T(4,128)S(1)} reduce(f32[4,1,21760]{2,1,0:T(1,128)S(1)} %all-to-all-done, f32[]{:T(128)} %broadcast.99), dimensions={1}, to_apply=%all_to_all.35.reduce_sub_computation | reduce | bytes 696324 | tf_op jit(solution)/shard_map/all_to_all | solution.py:16
  19.0 2.2 %reshape.91 = f32[1280,1,2,34]{3,2,1,0:T(2,128)S(1)} reshape(f32[4,21760]{1,0:T(4,128)S(1)} %reduce) | data formatting | bytes 696320
  21.3 1.3 %copy.30 = f32[1,34,2,4,320]{4,2,1,3,0:T(2,128)S(1)} copy(f32[1,34,2,4,320]{1,2,4,3,0:T(2,128)S(1)} %bitcast.70) | data formatting | bytes 696320 | tf_op jit(solution)/shard_map/all_to_all | solution.py:16
  23.6 1.0 %copy.32 = f32[1,136,2,320]{3,2,0,1:T(2,128)} copy(f32[1,136,2,320]{3,1,2,0:T(8,128)S(1)} %convolution_bitcast_fusion) | data formatting | bytes 696320 | tf_op jit(solution)/shard_map/lk,wkcn->wlcn/transpose | solution.py:24
  24.6 3.6 %all-to-all-start.1 = ((f32[1,136,2,320]{3,2,0,1:T(2,128)}), f32[1,136,2,320]{3,2,0,1:T(2,128)S(1)}, u32[]{:S(2)}, u32[]{:S(2)}) async-start(f32[1,136,2,320]{3,2,0,1:T(2,128)} %copy.32), calls=%async_computation.1 | async-start | bytes 835584 | tf_op jit(solution)/shard_map/all_to_all | solution.py:28
  28.2 0.7 dynamic_slice.11
  28.9 0.6 fusion.28
  29.5 6.4 %all-to-all-done.1 = f32[1,136,2,320]{3,2,0,1:T(2,128)S(1)} async-done(((f32[1,136,2,320]{3,2,0,1:T(2,128)}), f32[1,136,2,320]{3,2,0,1:T(2,128)S(1)}, u32[]{:S(2)}, u32[]{:S(2)}) %all-to-all-start.1) | async-done | bytes 348192 | tf_op jit(solution)/shard_map/all_to_all | solution.py:28
  36.3 0.8 convolution_bitcast_fusion.2
  37.1 0.7 reshape.92
  37.8 6.5 %all-to-all-start.2 = ((f32[8,1,136]{2,1,0:T(1,128)}), f32[8,1,136]{2,1,0:T(1,128)S(1)}, u32[]{:S(2)}, u32[]{:S(2)}) async-start(f32[8,1,136]{2,1,0:T(1,128)} %reshape.92), calls=%async_computation.2 | async-start | bytes 16384 | tf_op jit(solution)/shard_map/all_to_all | solution.py:33
  44.3 6.5 %all-to-all-done.2 = f32[8,1,136]{2,1,0:T(1,128)S(1)} async-done(((f32[8,1,136]{2,1,0:T(1,128)}), f32[8,1,136]{2,1,0:T(1,128)S(1)}, u32[]{:S(2)}, u32[]{:S(2)}) %all-to-all-start.2) | async-done | bytes 4384 | tf_op jit(solution)/shard_map/all_to_all | solution.py:33
  50.8 0.7 reduce.1
  51.6 26.6 %while.12 = (s32[]{:T(128)}, f32[2,34,5136]{2,0,1:T(2,128)S(1)}, f32[2,34,8,2]{1,2,3,0:T(8,128)S(1)}, s32[8]{0:T(128)S(1)}, s32[2]{0:T(128)S(1)}, /*index=5*/s32[]{:T(128)}, s32[]{:T(128)}) while((s32[]{:T(128)}, f32[2,34,5136]{2,0,1:T(2,128)S(1)}, f32[2,34,8,2]{1,2,3,0:T(8,128)S(1)}, s32[8]{0:T(128)S(1)}, ...), condition=%wide.region_1.2_spmd.clone.clone, body=%wide.region_0.1_spmd.clone.clone.sunk | while | flops 34329884 | bytes 4202137 | solution.py:50
  51.6 0.6 dynamic_slice.20
  53.5 0.6 compare_select_fusion.3
  54.8 2.3 %cosine_multiply_fusion.2 = (f32[8,5136]{1,0:T(8,128)S(1)}, f32[8,5136]{1,0:T(8,128)S(1)}) fusion(f32[8]{0:T(128)S(1)} %compare_select_fusion.3, f32[]{:T(128)S(6)} %convert_element_type.54, pred[]{:T(512)S(6)} %lt.78, s32[]{:T(128)S(6)} %select_n.59, s32[8]{0:T(128)S(1)} %get-tuple-element.139), kind=kLoop, calls=%fused_computation.15.clone.1 | loop fusion | flops 534144 | bytes 328777 | tf_op jit(solution)/shard_map/while/body/eval_jaxpr/mul | solution.py:44
  57.1 0.7 fusion.37
  57.8 0.9 %fusion.38 = f32[1,34,5136]{2,1,0:T(8,128)S(1)} fusion(f32[5136]{0:T(1024)S(1)} %fusion.37, f32[8,5136]{1,0:T(8,128)S(1)} %get-tuple-element.118, f32[8,5136]{1,0:T(8,128)S(1)} %get-tuple-element.119, f32[34,8]{0,1:T(8,128)S(1)} %get-tuple-element.120, f32[34,8]{0,1:T(8,128)S(1)} %get-tuple-element.121), kind=kOutput, calls=%fused_computation.2.clone.1 | convolution fusion | flops 33785152 | bytes 1049920 | tf_op jit(solution)/shard_map/while/body/eval_jaxpr/dot_general | solution.py:47
  58.7 0.7 copy.49
  59.4 5.3 %dynamic_update_slice.7 = f32[2,34,5136]{2,0,1:T(2,128)S(1)} dynamic-update-slice(f32[2,34,5136]{2,0,1:T(2,128)S(1)} %get-tuple-element.130, f32[1,34,5136]{2,0,1:T(1,128)S(1)} %copy.49, s32[]{:T(128)} %get-tuple-element.129, s32[]{:T(128)} %constant.25.clone.1..sunk, s32[]{:T(128)} %constant.25.clone.1..sunk) | dynamic-update-slice | bytes 1396996 | tf_op jit(solution)/shard_map/while/body/jit(dynamic_update_index_in_dim)/dynamic_update_slice | solution.py:50
  66.7 0.6 compare_select_fusion.3
  68.0 2.3 %cosine_multiply_fusion.2 = (f32[8,5136]{1,0:T(8,128)S(1)}, f32[8,5136]{1,0:T(8,128)S(1)}) fusion(f32[8]{0:T(128)S(1)} %compare_select_fusion.3, f32[]{:T(128)S(6)} %convert_element_type.54, pred[]{:T(512)S(6)} %lt.78, s32[]{:T(128)S(6)} %select_n.59, s32[8]{0:T(128)S(1)} %get-tuple-element.139), kind=kLoop, calls=%fused_computation.15.clone.1 | loop fusion | flops 534144 | bytes 328777 | tf_op jit(solution)/shard_map/while/body/eval_jaxpr/mul | solution.py:44
  70.3 0.7 fusion.37
  71.0 0.9 %fusion.38 = f32[1,34,5136]{2,1,0:T(8,128)S(1)} fusion(f32[5136]{0:T(1024)S(1)} %fusion.37, f32[8,5136]{1,0:T(8,128)S(1)} %get-tuple-element.118, f32[8,5136]{1,0:T(8,128)S(1)} %get-tuple-element.119, f32[34,8]{0,1:T(8,128)S(1)} %get-tuple-element.120, f32[34,8]{0,1:T(8,128)S(1)} %get-tuple-element.121), kind=kOutput, calls=%fused_computation.2.clone.1 | convolution fusion | flops 33785152 | bytes 1049920 | tf_op jit(solution)/shard_map/while/body/eval_jaxpr/dot_general | solution.py:47
  71.9 0.7 copy.49
  72.6 5.5 %dynamic_update_slice.7 = f32[2,34,5136]{2,0,1:T(2,128)S(1)} dynamic-update-slice(f32[2,34,5136]{2,0,1:T(2,128)S(1)} %get-tuple-element.130, f32[1,34,5136]{2,0,1:T(1,128)S(1)} %copy.49, s32[]{:T(128)} %get-tuple-element.129, s32[]{:T(128)} %constant.25.clone.1..sunk, s32[]{:T(128)} %constant.25.clone.1..sunk) | dynamic-update-slice | bytes 1396996 | tf_op jit(solution)/shard_map/while/body/jit(dynamic_update_index_in_dim)/dynamic_update_slice | solution.py:50
  78.1 1.1 %copy-done.5 = f32[2,34,5136]{2,0,1:T(2,128)} copy-done((f32[2,34,5136]{2,0,1:T(2,128)}, f32[2,34,5136]{2,0,1:T(2,128)S(1)}, u32[]{:S(2)}) %copy-start.5) | copy-done | bytes 1397016
  (29 shorter events, 2.8 us)
Async XLA Ops:
  0.0 22.5 %copy-start = (f32[136,136]{1,0:T(8,128)S(1)}, f32[136,136]{1,0:T(8,128)}, u32[]{:S(2)}) copy-start(f32[136,136]{1,0:T(8,128)} %param.10) | copy-start | bytes 221956
  2.6 7.3 %copy-start.4 = (f32[136]{0:T(256)S(1)}, f32[136]{0:T(256)}, u32[]{:S(2)}) copy-start(f32[136]{0:T(256)} %param.12) | copy-start | bytes 1636
  5.7 11.2 %all-to-all-start = ((f32[4,1,21760]{2,1,0:T(1,128)}), f32[4,1,21760]{2,1,0:T(1,128)S(1)}, u32[]{:S(2)}, u32[]{:S(2)}) async-start(f32[4,1,21760]{2,1,0:T(1,128)} %reshape.90), calls=%async_computation | async-start | bytes 696320 | tf_op jit(solution)/shard_map/all_to_all | solution.py:16
  21.3 1.8 %copy-start.1 = (f32[136,136]{1,0:T(8,128)S(1)}, f32[136,136]{1,0:T(8,128)}, u32[]{:S(2)}) copy-start(f32[136,136]{1,0:T(8,128)} %param.11) | copy-start | bytes 221956
  23.1 5.1 %copy-start.3 = (s32[8]{0:T(128)S(1)}, s32[8]{0:T(128)}, u32[]{:S(2)}) copy-start(s32[8]{0:T(128)} %param.14) | copy-start | bytes 100
  24.6 11.7 %copy-start.2 = (f32[1,16,1280]{2,1,0:T(8,128)S(1)}, f32[1,16,1280]{2,1,0:T(8,128)}, u32[]{:S(2)}) copy-start(f32[1,16,1280]{2,1,0:T(8,128)} %param.13) | copy-start | bytes 245764
  24.6 27.0 %copy-start.6 = (s32[2]{0:T(128)S(1)}, s32[2]{0:T(128)}, u32[]{:S(2)}) copy-start(s32[2]{0:T(128)} %param.15) | copy-start | bytes 28
  24.6 11.3 %all-to-all-start.1 = ((f32[1,136,2,320]{3,2,0,1:T(2,128)}), f32[1,136,2,320]{3,2,0,1:T(2,128)S(1)}, u32[]{:S(2)}, u32[]{:S(2)}) async-start(f32[1,136,2,320]{3,2,0,1:T(2,128)} %copy.32), calls=%async_computation.1 | async-start | bytes 835584 | tf_op jit(solution)/shard_map/all_to_all | solution.py:28
  37.8 13.0 %all-to-all-start.2 = ((f32[8,1,136]{2,1,0:T(1,128)}), f32[8,1,136]{2,1,0:T(1,128)S(1)}, u32[]{:S(2)}, u32[]{:S(2)}) async-start(f32[8,1,136]{2,1,0:T(1,128)} %reshape.92), calls=%async_computation.2 | async-start | bytes 16384 | tf_op jit(solution)/shard_map/all_to_all | solution.py:33
  78.1 1.1 %copy-start.5 = (f32[2,34,5136]{2,0,1:T(2,128)}, f32[2,34,5136]{2,0,1:T(2,128)S(1)}, u32[]{:S(2)}) copy-start(f32[2,34,5136]{2,0,1:T(2,128)S(1)} %get-tuple-element.40) | copy-start | bytes 4190980
where the time goes:
time: 79.7 us; the launch traced here: 79.2 us
  local copies, waits for them, and re-layouts  27.1 us (34%)
  waiting for transfers between devices  19.7 us (25%)
  starting transfers between devices  14.3 us (18%)
  other arithmetic  10.3 us (13%)
  loops' own time  4.04 us (5%)
  matrix products  3.55 us (4%)
    dynamic_update_slice x4, local copies, waits for them, and re-layouts, on_device(): lat_rows = lax.map(one_row, (jnp.moveaxis(band_data, 3, 0), lat_points))  12.3 us
    unnamed x19, local copies, waits for them, and re-layouts  9.8 us
    all_to_all x1, waiting for transfers between devices, on_device(): lax.all_to_all(spectral, 'lev', split_axis=3, concat_axis=1, tiled=True)  6.85 us
    all_to_all x1, waiting for transfers between devices, on_device(): lax.all_to_all(fourier, 'wave', split_axis=3, concat_axis=1, tiled=True)  6.51 us
    all_to_all x1, starting transfers between devices, on_device(): lax.all_to_all(fourier, 'wave', split_axis=3, concat_axis=1, tiled=True)  6.5 us
    all_to_all x1, waiting for transfers between devices, on_device(): lax.all_to_all(divergence, 'lev', split_axis=1, concat_axis=3, tiled=True)  6.37 us
    mul x2, other arithmetic, one_row(): jnp.cos(phases) * weight[:, None]  4.69 us
    all_to_all x1, starting transfers between devices, on_device(): lax.all_to_all(spectral, 'lev', split_axis=3, concat_axis=1, tiled=True)  4.21 us
  transfers between devices with their start and end apart: 3, of which 3 were waited for; matrix products, arithmetic and copies ran while one was open for 2% of the time, Pallas kernels for 0%

commit v1 on v0

--- a/solution.py
+++ b/solution.py
@@ -6,6 +6,18 @@
 
 LONS = 5136
 two_pi = 2.0 * math.pi
+
+
+def _meet_tables(a0, dim_at, u):
+    placed = a0.shape
+    d_next = a0.reshape(*placed[:dim_at], u, placed[dim_at] // u, *placed[dim_at + 1 :])
+    return jnp.moveaxis(d_next, dim_at, 0)
+
+
+def place_sides_all(page, array_dim):
+    local_next = list(page.shape[1:])
+    local_next[array_dim] *= page.shape[0]
+    return jnp.moveaxis(page, 0, array_dim).reshape(local_next)
 
 
 def on_device(spectral, to_modes, from_modes, mode_depths, legendre, wave_ids, lat_points):
@@ -30,7 +42,16 @@
     fourier = jnp.einsum(
         "wjn,wlcn->lwcj", legendre * keep_mask[:, None, :], level_major, precision=highest
     )
-    band_data = lax.all_to_all(fourier, "wave", split_axis=3, concat_axis=1, tiled=True)
+    oldest, g_now = (jax.lax.axis_size("wave"), jax.lax.axis_index("wave"))
+    work_now = _meet_tables(fourier, 3, oldest)
+    tray = [work_now[g_now]]
+    num = 1
+    while num < oldest:
+        wide_out = work_now[g_now ^ num]
+        tray.append(jax.lax.ppermute(wide_out, "wave", [(at, at ^ num) for at in range(oldest)]))
+        num += 1
+    work_now = jnp.stack(tray, 0)[g_now ^ jnp.arange(oldest)]
+    band_data = place_sides_all(work_now, 1)
     positions = jnp.arange(LONS)
 
     def one_row(inputs):

time: 79.7 us -> 84 us (1.054)
  starting transfers between devices: 14.3 us -> 19.6 us
    ppermute x0 -> x7, starting transfers between devices: none -> 11.7 us  [on_device(): jax.lax.ppermute(wide_out, 'wave', [(at, at ^ num) for at in range(oldest)])]
    all_to_all x1 -> x0, waiting for transfers between devices: 6.51 us -> none  [on_device(): lax.all_to_all(fourier, 'wave', split_axis=3, concat_axis=1, tiled=True)]
    all_to_all x1 -> x0, starting transfers between devices: 6.5 us -> none  [on_device(): lax.all_to_all(fourier, 'wave', split_axis=3, concat_axis=1, tiled=True)]
    ppermute x0 -> x7, waiting for transfers between devices: none -> 6.21 us  [on_device(): jax.lax.ppermute(wide_out, 'wave', [(at, at ^ num) for at in range(oldest)])]
    all_to_all x1, waiting for transfers between devices: 6.85 us -> 5.47 us  [on_device(): lax.all_to_all(spectral, 'lev', split_axis=3, concat_axis=1, tiled=True)]
    all_to_all x1, waiting for transfers between devices: 6.37 us -> 7.29 us  [on_device(): lax.all_to_all(divergence, 'lev', split_axis=1, concat_axis=3, tiled=True)]
    unnamed x19 -> x24, local copies, waits for them, and re-layouts: 9.8 us -> 9.07 us
  transfers between devices with their start and end apart: 3 -> 9, of which waited for: 3 -> 5; matrix products, arithmetic and copies ran while one was open for 2% -> 2% of each run, Pallas kernels for 0% -> 0%
where the time goes in v1:
time: 84 us; the launch traced here: 83.6 us
  local copies, waits for them, and re-layouts  27.4 us (33%)
  starting transfers between devices  19.6 us (23%)
  waiting for transfers between devices  19 us (23%)
  other arithmetic  9.74 us (12%)
  loops' own time  4.05 us (5%)
  matrix products  3.57 us (4%)
    dynamic_update_slice x4, local copies, waits for them, and re-layouts, on_device(): lat_rows = lax.map(one_row, (jnp.moveaxis(band_data, 3, 0), lat_points))  12.6 us
    ppermute x7, starting transfers between devices, on_device(): jax.lax.ppermute(wide_out, 'wave', [(at, at ^ num) for at in range(oldest)])  11.7 us
    unnamed x24, local copies, waits for them, and re-layouts  9.07 us
    all_to_all x1, waiting for transfers between devices, on_device(): lax.all_to_all(divergence, 'lev', split_axis=1, concat_axis=3, tiled=True)  7.29 us
    ppermute x7, waiting for transfers between devices, on_device(): jax.lax.ppermute(wide_out, 'wave', [(at, at ^ num) for at in range(oldest)])  6.21 us
    all_to_all x1, waiting for transfers between devices, on_device(): lax.all_to_all(spectral, 'lev', split_axis=3, concat_axis=1, tiled=True)  5.47 us
    mul x2, other arithmetic, one_row(): jnp.cos(phases) * weight[:, None]  4.69 us
    all_to_all x1, starting transfers between devices, on_device(): lax.all_to_all(spectral, 'lev', split_axis=3, concat_axis=1, tiled=True)  4.21 us
  transfers between devices with their start and end apart: 9, of which 5 were waited for; matrix products, arithmetic and copies ran while one was open for 2% of the time, Pallas kernels for 0%

profile of v1, /device:TPU:0, one launch (start us, length us, event | category | flops | bytes accessed | tf_op | source)
XLA Modules:
  0.0 83.6 jit_solution(6327551534290097055)
XLA Ops:
  0.0 2.6 %copy.30 = f32[1,34,2,1280]{1,2,0,3:T(2,128)S(1)} copy(f32[1,34,2,1280]{3,2,1,0:T(2,128)} %param.9) | data formatting | bytes 696320 | tf_op args[0]
  2.7 3.0 %reshape.157 = f32[4,1,21760]{2,1,0:T(1,128)} reshape(f32[1280,1,2,34]{3,2,1,0:T(2,128)S(1)} %bitcast.92) | data formatting | bytes 696320
  5.7 4.2 %all-to-all-start = ((f32[4,1,21760]{2,1,0:T(1,128)}), f32[4,1,21760]{2,1,0:T(1,128)S(1)}, u32[]{:S(2)}, u32[]{:S(2)}) async-start(f32[4,1,21760]{2,1,0:T(1,128)} %reshape.157), calls=%async_computation | async-start | bytes 696320 | tf_op jit(solution)/shard_map/all_to_all | solution.py:28
  9.9 0.7 dynamic_slice.11
  10.6 0.7 fusion.29
  11.4 5.5 %all-to-all-done = f32[4,1,21760]{2,1,0:T(1,128)S(1)} async-done(((f32[4,1,21760]{2,1,0:T(1,128)}), f32[4,1,21760]{2,1,0:T(1,128)S(1)}, u32[]{:S(2)}, u32[]{:S(2)}) %all-to-all-start) | async-done | bytes 348192 | tf_op jit(solution)/shard_map/all_to_all | solution.py:28
  17.4 1.6 %reduce = f32[4,21760]{1,0:T(4,128)S(1)} reduce(f32[4,1,21760]{2,1,0:T(1,128)S(1)} %all-to-all-done, f32[]{:T(128)} %broadcast.134), dimensions={1}, to_apply=%all_to_all.22.reduce_sub_computation | reduce | bytes 696324 | tf_op jit(solution)/shard_map/all_to_all | solution.py:28
  19.0 2.2 %reshape.158 = f32[1280,1,2,34]{3,2,1,0:T(2,128)S(1)} reshape(f32[4,21760]{1,0:T(4,128)S(1)} %reduce) | data formatting | bytes 696320
  21.3 1.3 %copy.31 = f32[1,34,2,4,320]{4,2,1,3,0:T(2,128)S(1)} copy(f32[1,34,2,4,320]{1,2,4,3,0:T(2,128)S(1)} %bitcast.91) | data formatting | bytes 696320 | tf_op jit(solution)/shard_map/all_to_all | solution.py:28
  23.6 1.0 %copy.33 = f32[1,136,2,320]{3,2,0,1:T(2,128)} copy(f32[1,136,2,320]{3,1,2,0:T(8,128)S(1)} %convolution_bitcast_fusion) | data formatting | bytes 696320 | tf_op jit(solution)/shard_map/lk,wkcn->wlcn/transpose | solution.py:36
  24.6 3.6 %all-to-all-start.1 = ((f32[1,136,2,320]{3,2,0,1:T(2,128)}), f32[1,136,2,320]{3,2,0,1:T(2,128)S(1)}, u32[]{:S(2)}, u32[]{:S(2)}) async-start(f32[1,136,2,320]{3,2,0,1:T(2,128)} %copy.33), calls=%async_computation.1 | async-start | bytes 835584 | tf_op jit(solution)/shard_map/all_to_all | solution.py:40
  28.4 7.3 %all-to-all-done.1 = f32[1,136,2,320]{3,2,0,1:T(2,128)S(1)} async-done(((f32[1,136,2,320]{3,2,0,1:T(2,128)}), f32[1,136,2,320]{3,2,0,1:T(2,128)S(1)}, u32[]{:S(2)}, u32[]{:S(2)}) %all-to-all-start.1) | async-done | bytes 348192 | tf_op jit(solution)/shard_map/all_to_all | solution.py:40
  36.1 0.8 fusion.23
  36.9 2.3 %collective-permute-start = (f32[34,1,2,2]{0,3,2,1:T(2,128)S(1)}, f32[34,1,2,2]{0,3,2,1:T(2,128)S(1)}, u32[]{:S(2)}, u32[]{:S(2)}) collective-permute-start(f32[34,1,2,2]{0,3,2,1:T(2,128)S(1)} %bitcast.104), channel_id=1, source_target_pairs={{0,4},{4,0},{8,12},{12,8},{16,20},{20,16},{24,28},{28,24},{1,5},{5... | collective-permute-start | bytes 1640 | tf_op jit(solution)/shard_map/ppermute | solution.py:51
  39.2 1.6 %collective-permute-start.1 = (f32[34,1,2,2]{0,3,2,1:T(2,128)S(1)}, f32[34,1,2,2]{0,3,2,1:T(2,128)S(1)}, u32[]{:S(2)}, u32[]{:S(2)}) collective-permute-start(f32[34,1,2,2]{0,3,2,1:T(2,128)S(1)} %bitcast.103), channel_id=1, source_target_pairs={{0,8},{4,12},{8,0},{12,4},{16,24},{20,28},{24,16},{28,20},{1,9},{5... | collective-permute-start | bytes 1640 | tf_op jit(solution)/shard_map/ppermute | solution.py:51
  40.8 3.0 %collective-permute-start.3 = (f32[34,1,2,2]{0,3,2,1:T(2,128)S(1)}, f32[34,1,2,2]{0,3,2,1:T(2,128)S(1)}, u32[]{:S(2)}, u32[]{:S(2)}) collective-permute-start(f32[34,1,2,2]{0,3,2,1:T(2,128)S(1)} %bitcast.101), channel_id=1, source_target_pairs={{0,16},{4,20},{8,24},{12,28},{16,0},{20,4},{24,8},{28,12},{1,17},{... | collective-permute-start | bytes 1640 | tf_op jit(solution)/shard_map/ppermute | solution.py:51
  43.8 1.3 %collective-permute-start.4 = (f32[34,1,2,2]{0,3,2,1:T(2,128)S(1)}, f32[34,1,2,2]{0,3,2,1:T(2,128)S(1)}, u32[]{:S(2)}, u32[]{:S(2)}) collective-permute-start(f32[34,1,2,2]{0,3,2,1:T(2,128)S(1)} %bitcast.100), channel_id=1, source_target_pairs={{0,20},{4,16},{8,28},{12,24},{16,4},{20,0},{24,12},{28,8},{1,21},{... | collective-permute-start | bytes 1640 | tf_op jit(solution)/shard_map/ppermute | solution.py:51
  45.1 3.6 %collective-permute-start.5 = (f32[34,1,2,2]{0,3,2,1:T(2,128)S(1)}, f32[34,1,2,2]{0,3,2,1:T(2,128)S(1)}, u32[]{:S(2)}, u32[]{:S(2)}) collective-permute-start(f32[34,1,2,2]{0,3,2,1:T(2,128)S(1)} %bitcast.99), channel_id=1, source_target_pairs={{0,24},{4,28},{8,16},{12,20},{16,8},{20,12},{24,0},{28,4},{1,25},{... | collective-permute-start | bytes 1640 | tf_op jit(solution)/shard_map/ppermute | solution.py:51
  49.2 1.3 %collective-permute-done.5 = f32[34,1,2,2]{0,3,2,1:T(2,128)S(1)} collective-permute-done((f32[34,1,2,2]{0,3,2,1:T(2,128)S(1)}, f32[34,1,2,2]{0,3,2,1:T(2,128)S(1)}, u32[]{:S(2)}, u32[]{:S(2)}) %collective-permute-start.5) | collective-permute-done | bytes 576 | tf_op jit(solution)/shard_map/ppermute | solution.py:51
  50.5 4.5 %collective-permute-done.6 = f32[34,1,2,2]{0,3,2,1:T(2,128)S(1)} collective-permute-done((f32[34,1,2,2]{0,3,2,1:T(2,128)S(1)}, f32[34,1,2,2]{0,3,2,1:T(2,128)S(1)}, u32[]{:S(2)}, u32[]{:S(2)}) %collective-permute-start.6) | collective-permute-done | bytes 576 | tf_op jit(solution)/shard_map/ppermute | solution.py:51
  55.5 26.9 %while.12 = (s32[]{:T(128)}, f32[2,34,5136]{2,0,1:T(2,128)S(1)}, f32[2,34,8,2]{1,0,3,2:T(2,128)S(1)}, s32[8]{0:T(128)S(1)}, s32[2]{0:T(128)S(1)}, /*index=5*/s32[]{:T(128)}, s32[]{:T(128)}) while((s32[]{:T(128)}, f32[2,34,5136]{2,0,1:T(2,128)S(1)}, f32[2,34,8,2]{1,0,3,2:T(2,128)S(1)}, s32[8]{0:T(128)S(1)}, ...), condition=%wide.region_1.2_spmd.clone.clone, body=%wide.region_0.1_spmd.clone.clone.sunk | while | flops 34329884 | bytes 4206489 | solution.py:71
  58.8 2.3 %cosine_multiply_fusion.2 = (f32[8,5136]{1,0:T(8,128)S(1)}, f32[8,5136]{1,0:T(8,128)S(1)}) fusion(f32[8]{0:T(128)S(1)} %compare_select_fusion.4, f32[]{:T(128)S(6)} %convert_element_type.54, pred[]{:T(512)S(6)} %lt.121, s32[]{:T(128)S(6)} %select_n.102, s32[8]{0:T(128)S(1)} %get-tuple-element.162), kind=kLoop, calls=%fused_computation.16.clone.1 | loop fusion | flops 534144 | bytes 328777 | tf_op jit(solution)/shard_map/while/body/eval_jaxpr/mul | solution.py:65
  61.1 0.7 fusion.38
  61.8 0.9 %fusion.39 = f32[1,34,5136]{2,1,0:T(8,128)S(1)} fusion(f32[5136]{0:T(1024)S(1)} %fusion.38, f32[8,5136]{1,0:T(8,128)S(1)} %get-tuple-element.141, f32[8,5136]{1,0:T(8,128)S(1)} %get-tuple-element.142, f32[34,8]{0,1:T(8,128)S(1)} %get-tuple-element.143, f32[34,8]{0,1:T(8,128)S(1)} %get-tuple-element.144), kind=kOutput, calls=%fused_computation.3.clone.1 | convolution fusion | flops 33785152 | bytes 1049920 | tf_op jit(solution)/shard_map/while/body/eval_jaxpr/dot_general | solution.py:68
  62.7 0.7 copy.56
  63.4 5.5 %dynamic_update_slice.7 = f32[2,34,5136]{2,0,1:T(2,128)S(1)} dynamic-update-slice(f32[2,34,5136]{2,0,1:T(2,128)S(1)} %get-tuple-element.153, f32[1,34,5136]{2,0,1:T(1,128)S(1)} %copy.56, s32[]{:T(128)} %get-tuple-element.152, s32[]{:T(128)} %constant.11.clone.1..sunk, s32[]{:T(128)} %constant.11.clone.1..sunk) | dynamic-update-slice | bytes 1396996 | tf_op jit(solution)/shard_map/while/body/jit(dynamic_update_index_in_dim)/dynamic_update_slice | solution.py:71
  72.1 2.3 %cosine_multiply_fusion.2 = (f32[8,5136]{1,0:T(8,128)S(1)}, f32[8,5136]{1,0:T(8,128)S(1)}) fusion(f32[8]{0:T(128)S(1)} %compare_select_fusion.4, f32[]{:T(128)S(6)} %convert_element_type.54, pred[]{:T(512)S(6)} %lt.121, s32[]{:T(128)S(6)} %select_n.102, s32[8]{0:T(128)S(1)} %get-tuple-element.162), kind=kLoop, calls=%fused_computation.16.clone.1 | loop fusion | flops 534144 | bytes 328777 | tf_op jit(solution)/shard_map/while/body/eval_jaxpr/mul | solution.py:65
  74.5 0.7 fusion.38
  75.2 0.9 %fusion.39 = f32[1,34,5136]{2,1,0:T(8,128)S(1)} fusion(f32[5136]{0:T(1024)S(1)} %fusion.38, f32[8,5136]{1,0:T(8,128)S(1)} %get-tuple-element.141, f32[8,5136]{1,0:T(8,128)S(1)} %get-tuple-element.142, f32[34,8]{0,1:T(8,128)S(1)} %get-tuple-element.143, f32[34,8]{0,1:T(8,128)S(1)} %get-tuple-element.144), kind=kOutput, calls=%fused_computation.3.clone.1 | convolution fusion | flops 33785152 | bytes 1049920 | tf_op jit(solution)/shard_map/while/body/eval_jaxpr/dot_general | solution.py:68
  76.1 0.7 copy.56
  76.8 5.7 %dynamic_update_slice.7 = f32[2,34,5136]{2,0,1:T(2,128)S(1)} dynamic-update-slice(f32[2,34,5136]{2,0,1:T(2,128)S(1)} %get-tuple-element.153, f32[1,34,5136]{2,0,1:T(1,128)S(1)} %copy.56, s32[]{:T(128)} %get-tuple-element.152, s32[]{:T(128)} %constant.11.clone.1..sunk, s32[]{:T(128)} %constant.11.clone.1..sunk) | dynamic-update-slice | bytes 1396996 | tf_op jit(solution)/shard_map/while/body/jit(dynamic_update_index_in_dim)/dynamic_update_slice | solution.py:71
  82.5 1.1 %copy-done.5 = f32[2,34,5136]{2,0,1:T(2,128)} copy-done((f32[2,34,5136]{2,0,1:T(2,128)}, f32[2,34,5136]{2,0,1:T(2,128)S(1)}, u32[]{:S(2)}) %copy-start.5) | copy-done | bytes 1397016
  (52 shorter events, 5.8 us)
Async XLA Ops:
  0.0 22.5 %copy-start = (f32[136,136]{1,0:T(8,128)S(1)}, f32[136,136]{1,0:T(8,128)}, u32[]{:S(2)}) copy-start(f32[136,136]{1,0:T(8,128)} %param.10) | copy-start | bytes 221956
  2.6 7.3 %copy-start.3 = (s32[8]{0:T(128)S(1)}, s32[8]{0:T(128)}, u32[]{:S(2)}) copy-start(s32[8]{0:T(128)} %param.14) | copy-start | bytes 100
  2.7 8.6 %copy-start.4 = (f32[136]{0:T(256)S(1)}, f32[136]{0:T(256)}, u32[]{:S(2)}) copy-start(f32[136]{0:T(256)} %param.12) | copy-start | bytes 1636
  5.7 11.2 %all-to-all-start = ((f32[4,1,21760]{2,1,0:T(1,128)}), f32[4,1,21760]{2,1,0:T(1,128)S(1)}, u32[]{:S(2)}, u32[]{:S(2)}) async-start(f32[4,1,21760]{2,1,0:T(1,128)} %reshape.157), calls=%async_computation | async-start | bytes 696320 | tf_op jit(solution)/shard_map/all_to_all | solution.py:28
  21.2 1.8 %copy-start.1 = (f32[136,136]{1,0:T(8,128)S(1)}, f32[136,136]{1,0:T(8,128)}, u32[]{:S(2)}) copy-start(f32[136,136]{1,0:T(8,128)} %param.11) | copy-start | bytes 221956
  23.1 5.2 %copy-start.2 = (f32[1,16,1280]{2,1,0:T(8,128)S(1)}, f32[1,16,1280]{2,1,0:T(8,128)}, u32[]{:S(2)}) copy-start(f32[1,16,1280]{2,1,0:T(8,128)} %param.13) | copy-start | bytes 245764
  24.6 11.1 %all-to-all-start.1 = ((f32[1,136,2,320]{3,2,0,1:T(2,128)}), f32[1,136,2,320]{3,2,0,1:T(2,128)S(1)}, u32[]{:S(2)}, u32[]{:S(2)}) async-start(f32[1,136,2,320]{3,2,0,1:T(2,128)} %copy.33), calls=%async_computation.1 | async-start | bytes 835584 | tf_op jit(solution)/shard_map/all_to_all | solution.py:40
  28.4 27.2 %copy-start.6 = (s32[2]{0:T(128)S(1)}, s32[2]{0:T(128)}, u32[]{:S(2)}) copy-start(s32[2]{0:T(128)} %param.15) | copy-start | bytes 28
  36.9 8.1 %collective-permute-start = (f32[34,1,2,2]{0,3,2,1:T(2,128)S(1)}, f32[34,1,2,2]{0,3,2,1:T(2,128)S(1)}, u32[]{:S(2)}, u32[]{:S(2)}) collective-permute-start(f32[34,1,2,2]{0,3,2,1:T(2,128)S(1)} %bitcast.104), channel_id=1, source_target_pairs={{0,4},{4,0},{8,12},{12,8},{16,20},{20,16},{24,28},{28,24},{1,5},{5... | collective-permute-start | bytes 1640 | tf_op jit(solution)/shard_map/ppermute | solution.py:51
  39.2 9.5 %collective-permute-start.1 = (f32[34,1,2,2]{0,3,2,1:T(2,128)S(1)}, f32[34,1,2,2]{0,3,2,1:T(2,128)S(1)}, u32[]{:S(2)}, u32[]{:S(2)}) collective-permute-start(f32[34,1,2,2]{0,3,2,1:T(2,128)S(1)} %bitcast.103), channel_id=1, source_target_pairs={{0,8},{4,12},{8,0},{12,4},{16,24},{20,28},{24,16},{28,20},{1,9},{5... | collective-permute-start | bytes 1640 | tf_op jit(solution)/shard_map/ppermute | solution.py:51
  40.8 7.9 %collective-permute-start.2 = (f32[34,1,2,2]{0,3,2,1:T(2,128)S(1)}, f32[34,1,2,2]{0,3,2,1:T(2,128)S(1)}, u32[]{:S(2)}, u32[]{:S(2)}) collective-permute-start(f32[34,1,2,2]{0,3,2,1:T(2,128)S(1)} %bitcast.102), channel_id=1, source_target_pairs={{0,12},{4,8},{8,4},{12,0},{16,28},{20,24},{24,20},{28,16},{1,13},{... | collective-permute-start | bytes 1640 | tf_op jit(solution)/shard_map/ppermute | solution.py:51
  40.8 7.9 %collective-permute-start.3 = (f32[34,1,2,2]{0,3,2,1:T(2,128)S(1)}, f32[34,1,2,2]{0,3,2,1:T(2,128)S(1)}, u32[]{:S(2)}, u32[]{:S(2)}) collective-permute-start(f32[34,1,2,2]{0,3,2,1:T(2,128)S(1)} %bitcast.101), channel_id=1, source_target_pairs={{0,16},{4,20},{8,24},{12,28},{16,0},{20,4},{24,8},{28,12},{1,17},{... | collective-permute-start | bytes 1640 | tf_op jit(solution)/shard_map/ppermute | solution.py:51
  43.8 5.4 %collective-permute-start.4 = (f32[34,1,2,2]{0,3,2,1:T(2,128)S(1)}, f32[34,1,2,2]{0,3,2,1:T(2,128)S(1)}, u32[]{:S(2)}, u32[]{:S(2)}) collective-permute-start(f32[34,1,2,2]{0,3,2,1:T(2,128)S(1)} %bitcast.100), channel_id=1, source_target_pairs={{0,20},{4,16},{8,28},{12,24},{16,4},{20,0},{24,12},{28,8},{1,21},{... | collective-permute-start | bytes 1640 | tf_op jit(solution)/shard_map/ppermute | solution.py:51
  45.1 5.4 %collective-permute-start.5 = (f32[34,1,2,2]{0,3,2,1:T(2,128)S(1)}, f32[34,1,2,2]{0,3,2,1:T(2,128)S(1)}, u32[]{:S(2)}, u32[]{:S(2)}) collective-permute-start(f32[34,1,2,2]{0,3,2,1:T(2,128)S(1)} %bitcast.99), channel_id=1, source_target_pairs={{0,24},{4,28},{8,16},{12,20},{16,8},{20,12},{24,0},{28,4},{1,25},{... | collective-permute-start | bytes 1640 | tf_op jit(solution)/shard_map/ppermute | solution.py:51
  48.7 6.3 %collective-permute-start.6 = (f32[34,1,2,2]{0,3,2,1:T(2,128)S(1)}, f32[34,1,2,2]{0,3,2,1:T(2,128)S(1)}, u32[]{:S(2)}, u32[]{:S(2)}) collective-permute-start(f32[34,1,2,2]{0,3,2,1:T(2,128)S(1)} %bitcast.98), channel_id=1, source_target_pairs={{0,28},{4,24},{8,20},{12,16},{16,12},{20,8},{24,4},{28,0},{1,29},{... | collective-permute-start | bytes 1640 | tf_op jit(solution)/shard_map/ppermute | solution.py:51
  82.5 1.1 %copy-start.5 = (f32[2,34,5136]{2,0,1:T(2,128)}, f32[2,34,5136]{2,0,1:T(2,128)S(1)}, u32[]{:S(2)}) copy-start(f32[2,34,5136]{2,0,1:T(2,128)S(1)} %get-tuple-element.40) | copy-start | bytes 4190980
